TPU v7x, 512 devices: a whole 4x8x8 slice. The times are simulated.
512 devices in a mesh: mode: 8 (over x, core), ax: 32 (over y, z_hi), rad: 2 (over z_lo).
Axes of the slice: x: 4, y: 8, z: 8 (z_hi: 4, z_lo: 2; z = z_hi * 2 + z_lo), core: 2. Of those that a mesh axis runs over, the one named last changes fastest.
Arguments:
- adjoint: float32 [5, 256, 128, 256], P(None, 'mode', 'ax', 'rad'), may hold values from -6 to 6
- state: float32 [5, 256, 128, 256], P(None, 'mode', 'ax', 'rad'), may hold values from -6 to 6
- wake: float32 [256, 128, 256], P('mode', 'ax', 'rad'), may hold values from 0.2 to 1.5
- jac_axial: float32 [5, 5], replicated, may hold values from -2.5 to 2.5
- jac_radial: float32 [5, 5], replicated, may hold values from -2.5 to 2.5
- jac_swirl: float32 [5, 5], replicated, may hold values from -2.5 to 2.5
- wake_coupling: float32 [5, 5], replicated, may hold values from -2.5 to 2.5
Outputs:
- adjoint_in: float32 [5, 256, 128, 256], P(None, 'mode', 'ax', 'rad')
- wake_grad: float32 [256, 128, 256], P('mode', 'ax', 'rad')
All inputs are finite; a program needn't handle non-finite values.
Results may differ from a plain program's by a relative error of at most 0.000098.
Values sent between devices are 32-bit elements; how exact they have to be, the bound alone decides.
A program may use at most 64 MiB of HBM per device.

v0:
```python
import functools
import math

import jax
import jax.numpy as jnp
import ml_dtypes
import numpy as np
from jax import lax
from jax.experimental import pallas as pl
from jax.experimental.pallas import tpu as pltpu
from jax.sharding import PartitionSpec as P

MESH = pl.DeviceIdType.MESH
F, K, X, L = 5, 32, 4, 128
D = 8
HALF = L // 2
PAIRS = 3
ORDER = (4, 5, 3, 2, 6, 7, 1)


def basis_parts():
    t = np.arange(D * K)[:, None]
    k = np.arange(D * K)[None, :]
    phase = ((k // 2) * t % (D * K)) * (2.0 * math.pi / (D * K))
    table = math.sqrt(2.0 / (D * K)) * np.where(k % 2 == 0, np.cos(phase), np.sin(phase))
    one = 1.0 / math.sqrt(D * K)
    table = np.where(k == 0, one, table)
    table = np.where(k == 1, np.where(t % 2 == 0, one, -one), table)
    high = table.astype(ml_dtypes.bfloat16)
    low = (table - high.astype(np.float64)).astype(ml_dtypes.bfloat16)
    return high, low


def product(high, low, x):
    x_high = x.astype(jnp.bfloat16)
    x_low = (x - x_high.astype(jnp.float32)).astype(jnp.bfloat16)
    dot = functools.partial(jnp.dot, preferred_element_type=jnp.float32)
    return dot(high, x_high) + (dot(high, x_low) + dot(low, x_high))


def kernel(
    adj_hbm, state_hbm, wake_hbm, bh_hbm, bl_hbm, th_hbm, tl_hbm, ja_hbm, jr_hbm, js_hbm, wc_hbm,
    out_ref, grad_ref,
    adj_ref, state_ref, wake_ref, bh_ref, bl_ref, th_ref, tl_ref, ja_ref, jr_ref, js_ref, wc_ref, in_sem,
    send, recv, wsend, wrecv, wfull, back, ret, hsend, hrecv, esend, erecv, acc,
    f_ssem, f_rsem, w_ssem, w_rsem, b_ssem, b_rsem, h_ssem, h_rsem, e_ssem, e_rsem,
):
    me = lax.axis_index("mode")
    ax = lax.axis_index("ax")
    rad = lax.axis_index("rad")
    ax_count = lax.axis_size("ax")
    ax_up = lax.rem(ax + 1, ax_count)
    ax_down = lax.rem(ax + ax_count - 1, ax_count)
    others = [lax.rem(me + i, D) for i in ORDER]

    barrier = pltpu.get_barrier_semaphore()
    for other in others:
        pl.semaphore_signal(barrier, inc=1, device_id={"mode": other}, device_id_type=MESH)
    pl.semaphore_signal(barrier, inc=1, device_id={"ax": ax_up}, device_id_type=MESH)
    pl.semaphore_signal(barrier, inc=1, device_id={"ax": ax_down}, device_id_type=MESH)
    pl.semaphore_signal(barrier, inc=1, device_id={"rad": 1 - rad}, device_id_type=MESH)

    sources = (adj_hbm, state_hbm, wake_hbm, bh_hbm, bl_hbm, th_hbm, tl_hbm, ja_hbm, jr_hbm, js_hbm, wc_hbm)
    targets = (adj_ref, state_ref, wake_ref, bh_ref, bl_ref, th_ref, tl_ref, ja_ref, jr_ref, js_ref, wc_ref)
    loads = [pltpu.make_async_copy(a, b, in_sem.at[i]) for i, (a, b) in enumerate(zip(sources, targets))]
    for i in (10, 1, 0, 2, 3, 4, 5, 6, 7, 8, 9):
        loads[i].start()

    lane = lax.broadcasted_iota(jnp.int32, (K, L), 1)
    low_half = lane < HALF

    def cells(ref, f, x):
        return ref[f, pl.ds(x, K, stride=X), :]

    def swap(v):
        return pltpu.roll(v, HALF, axis=1)

    started = []

    def go(src, dst, ssem, rsem, device):
        copy = pltpu.make_async_remote_copy(
            src_ref=src, dst_ref=dst, send_sem=ssem, recv_sem=rsem, device_id=device, device_id_type=MESH
        )
        copy.start()
        started.append(copy)

    for i in (10, 1, 0):
        loads[i].wait()
    q = K // 2
    for f in range(F):
        for x in range(X):
            a = cells(adj_ref, f, x)
            c = wc_ref[f, 0] * cells(state_ref, 0, x)
            for e in range(1, F):
                c = c + wc_ref[f, e] * cells(state_ref, e, x)
            send[f, 2 * x] = jnp.where(low_half, a, swap(c))
            send[f, 2 * x + 1] = jnp.where(low_half, swap(a), c)
        if f == 0:
            loads[2].wait()
            for x in range(X):
                w = wake_ref[pl.ds(x, K, stride=X), :]
                w_swap = swap(w)
                m = low_half[:q]
                wsend[2 * x] = jnp.where(m, w[:q], w_swap[q:])
                wsend[2 * x + 1] = jnp.where(m, w_swap[:q], w[q:])
            pl.semaphore_wait(barrier, D + 2)
        for other in others:
            go(send.at[f, other], recv.at[f, me], f_ssem.at[f, other], f_rsem.at[f, me], {"mode": other})
        if f == 0:
            for other in others:
                go(wsend.at[other], wrecv.at[me], w_ssem.at[other], w_rsem.at[me], {"mode": other})

    edge = jnp.zeros((K, L), jnp.float32)
    for f in range(F):
        hsend[0, f] = cells(adj_ref, f, 0)
        hsend[1, f] = cells(adj_ref, f, X - 1)
        for x in range(X):
            s = f * X + x
            v = cells(adj_ref, f, x)
            v = jnp.where(rad == 0, pltpu.roll(v, s + 1, axis=1), pltpu.roll(v, s, axis=1) if s else v)
            edge = jnp.where(lane == s, v, edge)
    esend[...] = edge
    go(hsend.at[0], hrecv.at[1], h_ssem.at[0], h_rsem.at[1], {"ax": ax_down})
    go(hsend.at[1], hrecv.at[0], h_ssem.at[1], h_rsem.at[0], {"ax": ax_up})
    go(esend, erecv, e_ssem, e_rsem, {"rad": 1 - rad})

    wrecv[me] = wsend[me]
    for f in range(F):
        recv[f, me] = send[f, me]

    def arrived(ref, sem):
        pltpu.make_async_remote_copy(
            src_ref=ref, dst_ref=ref, send_sem=sem, recv_sem=sem, device_id={"mode": me}, device_id_type=MESH
        ).wait_recv()

    for other in others:
        arrived(wrecv.at[other], w_rsem.at[other])
    for d in range(D):
        w = wrecv[d]
        w_swap = swap(w)
        m = low_half[:q]
        wfull[pl.ds(d * K, q), :] = jnp.where(m, w, w_swap)
        wfull[pl.ds(d * K + q, q), :] = jnp.where(m, w_swap, w)

    for i in (3, 4, 5, 6, 7, 8, 9):
        loads[i].wait()
    low_all = lax.broadcasted_iota(jnp.int32, (D * K, L), 1) < HALF
    total = None
    first = None
    for f in range(F):
        for other in others:
            arrived(recv.at[f, other], f_rsem.at[f, other])
        angle = product(bh_ref[...], bl_ref[...], recv[f].reshape(D * K, L))
        angle_swap = swap(angle)
        term = angle * angle_swap
        total = term if total is None else total + term
        wake_all = wfull[...]
        if f % 2 == 0 and f < F - 1:
            first = wake_all * angle
            continue
        p = f // 2
        if f < F - 1:
            both = jnp.where(low_all, first, wake_all * angle_swap)
        else:
            both = wake_all * angle
        result = product(th_ref[...], tl_ref[...], both)
        if f == F - 1:
            result = jnp.where(low_all, result, -total)
        back[p] = result.reshape(D, K, L)
        for other in others:
            go(back.at[p, other], ret.at[p, me], b_ssem.at[p, other], b_rsem.at[p, me], {"mode": other})
        ret[p, me] = back[p, me]

    arrived(hrecv.at[0], h_rsem.at[0])
    arrived(hrecv.at[1], h_rsem.at[1])
    arrived(erecv, e_rsem)
    row = lax.broadcasted_iota(jnp.int32, (K, L), 0)
    even = lax.rem(row, 2) == 0
    order = lax.div(me * K + row, 2).astype(jnp.float32) / jnp.float32(D * K // 2)
    radius = 0.5 + ((rad * L + lane).astype(jnp.float32) + 0.5) / jnp.float32(4.0 * L)
    rate = (0.25 / radius) * order
    rate = jnp.where(even, rate, -rate)
    nearby = erecv[...]
    nearby_up = jnp.where(rad == 0, nearby, 0.0)
    nearby_down = jnp.where(rad == 1, nearby, 0.0)
    for x in range(X):
        fields, axial, radial, turned = [], [], [], []
        for e in range(F):
            a = cells(adj_ref, e, x)
            fields.append(a)
            if x == X - 1:
                above = jnp.where(ax < ax_count - 1, hrecv[1, e], 0.0)
            else:
                above = cells(adj_ref, e, x + 1)
            if x == 0:
                below = jnp.where(ax > 0, hrecv[0, e], 0.0)
            else:
                below = cells(adj_ref, e, x - 1)
            axial.append(0.5 * (above - below))
            s = e * X + x
            up = jnp.where(lane == L - 1, pltpu.roll(nearby_up, L - 1 - s, axis=1), pltpu.roll(a, L - 1, axis=1))
            edge_down = pltpu.roll(nearby_down, L - s, axis=1) if s else nearby_down
            down = jnp.where(lane == 0, edge_down, pltpu.roll(a, 1, axis=1))
            radial.append(0.5 * (up - down))
            turned.append(rate * jnp.where(even, pltpu.roll(a, K - 1, axis=0), pltpu.roll(a, 1, axis=0)))
        for f in range(F):
            v = fields[f]
            for e in range(F):
                v = v + ja_ref[e, f] * axial[e] + jr_ref[e, f] * radial[e] + js_ref[e, f] * turned[e]
            acc[f, x] = v

    for p in range(PAIRS):
        for other in others:
            arrived(ret.at[p, other], b_rsem.at[p, other])
    for x in range(X):
        returned = []
        for p in range(PAIRS):
            one, two = ret[p, 2 * x], ret[p, 2 * x + 1]
            returned.append(jnp.where(low_half, one, swap(two)))
            returned.append(jnp.where(low_half, swap(one), two))
        grad_ref[pl.ds(x, K, stride=X), :] = returned[F]
        for f in range(F):
            v = acc[f, x]
            for e in range(F):
                v = v - wc_ref[e, f] * returned[e]
            out_ref[f, pl.ds(x, K, stride=X), :] = v

    for copy in started:
        copy.wait_send()


def body(adjoint, state, wake, jac_axial, jac_radial, jac_swirl, wake_coupling):
    high, low = basis_parts()
    vmem = pl.BlockSpec(memory_space=pltpu.VMEM)
    hbm = pl.BlockSpec(memory_space=pltpu.HBM)
    dma = pltpu.SemaphoreType.DMA
    f32 = jnp.float32
    adjoint_in, grad = pl.pallas_call(
        kernel,
        out_shape=(
            jax.ShapeDtypeStruct((F, K * X, L), f32),
            jax.ShapeDtypeStruct((K * X, L), f32),
        ),
        in_specs=[hbm] * 11,
        out_specs=(vmem, vmem),
        scratch_shapes=[
            pltpu.VMEM((F, K * X, L), f32),
            pltpu.VMEM((F, K * X, L), f32),
            pltpu.VMEM((K * X, L), f32),
            *[pltpu.VMEM((D * K, D * K), jnp.bfloat16)] * 4,
            *[pltpu.SMEM((F, F), f32)] * 4,
            dma((11,)),
            pltpu.VMEM((F, D, K, L), f32),
            pltpu.VMEM((F, D, K, L), f32),
            pltpu.VMEM((D, K // 2, L), f32),
            pltpu.VMEM((D, K // 2, L), f32),
            pltpu.VMEM((D * K, L), f32),
            pltpu.VMEM((PAIRS, D, K, L), f32),
            pltpu.VMEM((PAIRS, D, K, L), f32),
            pltpu.VMEM((2, F, K, L), f32),
            pltpu.VMEM((2, F, K, L), f32),
            pltpu.VMEM((K, L), f32),
            pltpu.VMEM((K, L), f32),
            pltpu.VMEM((F, X, K, L), f32),
            dma((F, D)), dma((F, D)), dma((D,)), dma((D,)), dma((PAIRS, D)), dma((PAIRS, D)),
            dma((2,)), dma((2,)), dma, dma,
        ],
        compiler_params=pltpu.CompilerParams(
            collective_id=0, has_side_effects=True, vmem_limit_bytes=32 * 1024 * 1024
        ),
        name="section_adjoint",
    )(
        *[pltpu.with_memory_space_constraint(v, pltpu.HBM) for v in (adjoint.reshape(F, K * X, L), state.reshape(F, K * X, L), wake.reshape(K * X, L),
        jnp.asarray(high), jnp.asarray(low), jnp.asarray(np.ascontiguousarray(high.T)),
        jnp.asarray(np.ascontiguousarray(low.T)), jac_axial, jac_radial, jac_swirl, wake_coupling)],
    )
    return adjoint_in.reshape(adjoint.shape), grad.reshape(wake.shape)


def solution(mesh):
    return jax.shard_map(
        body,
        mesh=mesh,
        in_specs=(
            P(None, "mode", "ax", "rad"),
            P(None, "mode", "ax", "rad"),
            P("mode", "ax", "rad"),
            P(),
            P(),
            P(),
            P(),
        ),
        out_specs=(P(None, "mode", "ax", "rad"), P("mode", "ax", "rad")),
        check_vma=False,
    )
```

profile of v0, /device:TPU:1, one launch (start us, length us, event | category | flops | bytes accessed | tf_op | source)
XLA Modules:
  0.0 32.9 jit_solution(6537354010542396686)
XLA Ops:
  0.6 30.9 %section_adjoint.1 = (f32[5,128,128]{2,1,0:T(8,128)S(1)}, f32[128,128]{1,0:T(8,128)S(1)}) custom-call(f32[5,128,128]{2,1,0:T(8,128)} %bitcast.7, f32[5,128,128]{2,1,0:T(8,128)} %bitcast.8, f32[128,128]{1,0:T(8,128)} %bitcast.9, bf16[256,256]{1,0:T(8,128)(2,1)} %constant.8.clone.bh_hbm, bf16[256,256]{1,0:T(8,128)(2,1)} %constant.9.clone.bl_hbm, ...), custom_call_target="tpu_custom_call" | custom-call | tf_op jit(solution)/shard_map/section_adjoint/pallas_call | solution.py:238
  31.6 0.7 %copy.15 = f32[5,32,4,128]{3,2,1,0:T(4,128)} copy(f32[5,32,4,128]{3,2,1,0:T(4,128)S(1)} %bitcast.5) | data formatting | bytes 655360
  32.3 0.6 %copy.16 = f32[32,4,128]{2,1,0:T(4,128)} copy(f32[32,4,128]{2,1,0:T(4,128)S(1)} %bitcast.6) | data formatting | bytes 131072
where the time goes:
time: 33.1 us; the launch traced here: 32.9 us
  Pallas kernels  30.9 us (93%)
  local copies, waits for them, and re-layouts  1.36 us (4%)
  between operations  0.64 us (2%)
    pallas_call x1, Pallas kernels, body(): pl.pallas_call(kernel, out_shape=(jax.ShapeDtypeStruct((F, K * X, L), f32...  30.9 us
    unnamed x2, local copies, waits for them, and re-layouts  1.36 us

commit v1 on v0

--- a/solution.py
+++ b/solution.py
@@ -49,15 +49,22 @@
     ax = lax.axis_index("ax")
     rad = lax.axis_index("rad")
     ax_count = lax.axis_size("ax")
-    ax_up = lax.rem(ax + 1, ax_count)
-    ax_down = lax.rem(ax + ax_count - 1, ax_count)
+    has_up = ax < ax_count - 1
+    has_down = ax > 0
     others = [lax.rem(me + i, D) for i in ORDER]
 
     barrier = pltpu.get_barrier_semaphore()
     for other in others:
         pl.semaphore_signal(barrier, inc=1, device_id={"mode": other}, device_id_type=MESH)
-    pl.semaphore_signal(barrier, inc=1, device_id={"ax": ax_up}, device_id_type=MESH)
-    pl.semaphore_signal(barrier, inc=1, device_id={"ax": ax_down}, device_id_type=MESH)
+
+    @pl.when(has_up)
+    def _():
+        pl.semaphore_signal(barrier, inc=1, device_id={"ax": ax + 1}, device_id_type=MESH)
+
+    @pl.when(has_down)
+    def _():
+        pl.semaphore_signal(barrier, inc=1, device_id={"ax": ax - 1}, device_id_type=MESH)
+
     pl.semaphore_signal(barrier, inc=1, device_id={"rad": 1 - rad}, device_id_type=MESH)
 
     sources = (adj_hbm, state_hbm, wake_hbm, bh_hbm, bl_hbm, th_hbm, tl_hbm, ja_hbm, jr_hbm, js_hbm, wc_hbm)
@@ -75,14 +82,12 @@
     def swap(v):
         return pltpu.roll(v, HALF, axis=1)
 
-    started = []
-
     def go(src, dst, ssem, rsem, device):
         copy = pltpu.make_async_remote_copy(
             src_ref=src, dst_ref=dst, send_sem=ssem, recv_sem=rsem, device_id=device, device_id_type=MESH
         )
         copy.start()
-        started.append(copy)
+        return copy
 
     for i in (10, 1, 0):
         loads[i].wait()
@@ -103,12 +108,12 @@
                 m = low_half[:q]
                 wsend[2 * x] = jnp.where(m, w[:q], w_swap[q:])
                 wsend[2 * x + 1] = jnp.where(m, w_swap[:q], w[q:])
-            pl.semaphore_wait(barrier, D + 2)
+            pl.semaphore_wait(barrier, D + has_up.astype(jnp.int32) + has_down.astype(jnp.int32))
         for other in others:
-            go(send.at[f, other], recv.at[f, me], f_ssem.at[f, other], f_rsem.at[f, me], {"mode": other})
+            go(send.at[f, other], recv.at[f, me], f_ssem.at[f], f_rsem.at[f], {"mode": other})
         if f == 0:
             for other in others:
-                go(wsend.at[other], wrecv.at[me], w_ssem.at[other], w_rsem.at[me], {"mode": other})
+                go(wsend.at[other], wrecv.at[me], w_ssem, w_rsem, {"mode": other})
 
     edge = jnp.zeros((K, L), jnp.float32)
     for f in range(F):
@@ -120,21 +125,29 @@
             v = jnp.where(rad == 0, pltpu.roll(v, s + 1, axis=1), pltpu.roll(v, s, axis=1) if s else v)
             edge = jnp.where(lane == s, v, edge)
     esend[...] = edge
-    go(hsend.at[0], hrecv.at[1], h_ssem.at[0], h_rsem.at[1], {"ax": ax_down})
-    go(hsend.at[1], hrecv.at[0], h_ssem.at[1], h_rsem.at[0], {"ax": ax_up})
+
+    @pl.when(has_down)
+    def _():
+        go(hsend.at[0], hrecv.at[1], h_ssem.at[0], h_rsem.at[1], {"ax": ax - 1})
+
+    @pl.when(has_up)
+    def _():
+        go(hsend.at[1], hrecv.at[0], h_ssem.at[1], h_rsem.at[0], {"ax": ax + 1})
+
     go(esend, erecv, e_ssem, e_rsem, {"rad": 1 - rad})
 
     wrecv[me] = wsend[me]
     for f in range(F):
         recv[f, me] = send[f, me]
 
-    def arrived(ref, sem):
-        pltpu.make_async_remote_copy(
-            src_ref=ref, dst_ref=ref, send_sem=sem, recv_sem=sem, device_id={"mode": me}, device_id_type=MESH
-        ).wait_recv()
-
-    for other in others:
-        arrived(wrecv.at[other], w_rsem.at[other])
+    def whole(ref, sem):
+        return pltpu.make_async_remote_copy(
+            src_ref=ref, dst_ref=ref, send_sem=sem, recv_sem=sem, device_id={"rad": 1 - rad}, device_id_type=MESH
+        )
+
+    seven = pl.ds(0, D - 1)
+
+    whole(wrecv.at[seven], w_rsem).wait_recv()
     for d in range(D):
         w = wrecv[d]
         w_swap = swap(w)
@@ -148,8 +161,7 @@
     total = None
     first = None
     for f in range(F):
-        for other in others:
-            arrived(recv.at[f, other], f_rsem.at[f, other])
+        whole(recv.at[f, seven], f_rsem.at[f]).wait_recv()
         angle = product(bh_ref[...], bl_ref[...], recv[f].reshape(D * K, L))
         angle_swap = swap(angle)
         term = angle * angle_swap
@@ -168,12 +180,24 @@
             result = jnp.where(low_all, result, -total)
         back[p] = result.reshape(D, K, L)
         for other in others:
-            go(back.at[p, other], ret.at[p, me], b_ssem.at[p, other], b_rsem.at[p, me], {"mode": other})
+            go(back.at[p, other], ret.at[p, me], b_ssem.at[p], b_rsem.at[p], {"mode": other})
         ret[p, me] = back[p, me]
 
-    arrived(hrecv.at[0], h_rsem.at[0])
-    arrived(hrecv.at[1], h_rsem.at[1])
-    arrived(erecv, e_rsem)
+    @pl.when(has_down)
+    def _():
+        whole(hrecv.at[0], h_rsem.at[0]).wait_recv()
+        whole(hsend.at[0], h_ssem.at[0]).wait_send()
+
+    @pl.when(has_up)
+    def _():
+        whole(hrecv.at[1], h_rsem.at[1]).wait_recv()
+        whole(hsend.at[1], h_ssem.at[1]).wait_send()
+
+    whole(erecv, e_rsem).wait_recv()
+    whole(esend, e_ssem).wait_send()
+    whole(wsend.at[seven], w_ssem).wait_send()
+    for f in range(F):
+        whole(send.at[f, seven], f_ssem.at[f]).wait_send()
     row = lax.broadcasted_iota(jnp.int32, (K, L), 0)
     even = lax.rem(row, 2) == 0
     order = lax.div(me * K + row, 2).astype(jnp.float32) / jnp.float32(D * K // 2)
@@ -189,11 +213,11 @@
             a = cells(adj_ref, e, x)
             fields.append(a)
             if x == X - 1:
-                above = jnp.where(ax < ax_count - 1, hrecv[1, e], 0.0)
+                above = jnp.where(has_up, hrecv[1, e], 0.0)
             else:
                 above = cells(adj_ref, e, x + 1)
             if x == 0:
-                below = jnp.where(ax > 0, hrecv[0, e], 0.0)
+                below = jnp.where(has_down, hrecv[0, e], 0.0)
             else:
                 below = cells(adj_ref, e, x - 1)
             axial.append(0.5 * (above - below))
@@ -209,24 +233,39 @@
                 v = v + ja_ref[e, f] * axial[e] + jr_ref[e, f] * radial[e] + js_ref[e, f] * turned[e]
             acc[f, x] = v
 
-    for p in range(PAIRS):
-        for other in others:
-            arrived(ret.at[p, other], b_rsem.at[p, other])
+    def pair(p, x):
+        one, two = ret[p, 2 * x], ret[p, 2 * x + 1]
+        return jnp.where(low_half, one, swap(two)), jnp.where(low_half, swap(one), two)
+
+    for p in range(PAIRS - 1):
+        whole(ret.at[p, seven], b_rsem.at[p]).wait_recv()
+        whole(back.at[p, seven], b_ssem.at[p]).wait_send()
     for x in range(X):
-        returned = []
-        for p in range(PAIRS):
-            one, two = ret[p, 2 * x], ret[p, 2 * x + 1]
-            returned.append(jnp.where(low_half, one, swap(two)))
-            returned.append(jnp.where(low_half, swap(one), two))
-        grad_ref[pl.ds(x, K, stride=X), :] = returned[F]
+        returned = [v for p in range(PAIRS - 1) for v in pair(p, x)]
         for f in range(F):
             v = acc[f, x]
-            for e in range(F):
+            for e in range(F - 1):
                 v = v - wc_ref[e, f] * returned[e]
-            out_ref[f, pl.ds(x, K, stride=X), :] = v
-
-    for copy in started:
-        copy.wait_send()
+            acc[f, x] = v
+    p = PAIRS - 1
+    whole(back.at[p, seven], b_ssem.at[p]).wait_send()
+    whole(ret.at[p, seven], b_rsem.at[p]).wait_recv()
+    for x in range(X):
+        last, grad = pair(p, x)
+        grad_ref[pl.ds(x, K, stride=X), :] = grad
+        for f in range(F):
+            out_ref[f, pl.ds(x, K, stride=X), :] = acc[f, x] - wc_ref[F - 1, f] * last
+
+
+def write_out(field_ref, grad_ref, field_out, grad_out, sem):
+    copies = [
+        pltpu.make_async_copy(field_ref, field_out, sem.at[0]),
+        pltpu.make_async_copy(grad_ref, grad_out, sem.at[1]),
+    ]
+    for copy in copies:
+        copy.start()
+    for copy in copies:
+        copy.wait()
 
 
 def body(adjoint, state, wake, jac_axial, jac_radial, jac_swirl, wake_coupling):
@@ -262,7 +301,7 @@
             pltpu.VMEM((K, L), f32),
             pltpu.VMEM((K, L), f32),
             pltpu.VMEM((F, X, K, L), f32),
-            dma((F, D)), dma((F, D)), dma((D,)), dma((D,)), dma((PAIRS, D)), dma((PAIRS, D)),
+            dma((F,)), dma((F,)), dma, dma, dma((PAIRS,)), dma((PAIRS,)),
             dma((2,)), dma((2,)), dma, dma,
         ],
         compiler_params=pltpu.CompilerParams(
@@ -274,6 +313,18 @@
         jnp.asarray(high), jnp.asarray(low), jnp.asarray(np.ascontiguousarray(high.T)),
         jnp.asarray(np.ascontiguousarray(low.T)), jac_axial, jac_radial, jac_swirl, wake_coupling)],
     )
+    adjoint_in, grad = pl.pallas_call(
+        write_out,
+        out_shape=(
+            jax.ShapeDtypeStruct((F, K * X, L), f32),
+            jax.ShapeDtypeStruct((K * X, L), f32),
+        ),
+        in_specs=[vmem] * 2,
+        out_specs=(hbm, hbm),
+        scratch_shapes=[dma((2,))],
+        compiler_params=pltpu.CompilerParams(vmem_limit_bytes=1024 * 1024),
+        name="write_out",
+    )(adjoint_in, grad)
     return adjoint_in.reshape(adjoint.shape), grad.reshape(wake.shape)
 
 

time: 33.1 us -> 28.2 us (0.85)
  the two profiles are of different devices: /device:TPU:1 before, /device:TPU:40 now
where the time goes in v1:
time: 28.2 us; the launch traced here: 28.1 us
  Pallas kernels  27.4 us (97%)
  between operations  0.64 us (2%)
    pallas_call x1, Pallas kernels, body(): pl.pallas_call(kernel, out_shape=(jax.ShapeDtypeStruct((F, K * X, L), f32...  26.7 us
    pallas_call x1, Pallas kernels, body(): pl.pallas_call(write_out, out_shape=(jax.ShapeDtypeStruct((F, K * X, L),...  0.76 us

profile of v1, /device:TPU:40, one launch (start us, length us, event | category | flops | bytes accessed | tf_op | source)
XLA Modules:
  0.0 28.1 jit_solution(3778399537531101055)
XLA Ops:
  0.6 26.7 %section_adjoint.1 = (f32[5,128,128]{2,1,0:T(8,128)S(1)}, f32[128,128]{1,0:T(8,128)S(1)}) custom-call(f32[5,128,128]{2,1,0:T(8,128)} %bitcast.5, f32[5,128,128]{2,1,0:T(8,128)} %bitcast.6, f32[128,128]{1,0:T(8,128)} %bitcast.7, bf16[256,256]{1,0:T(8,128)(2,1)} %constant.8.clone.bh_hbm, bf16[256,256]{1,0:T(8,128)(2,1)} %constant.9.clone.bl_hbm, ...), custom_call_target="tpu_custom_call" | custom-call | tf_op jit(solution)/shard_map/section_adjoint/pallas_call | solution.py:277
  27.3 0.8 %write_out.1 = (f32[5,128,128]{2,1,0:T(8,128)}, f32[128,128]{1,0:T(8,128)}) custom-call(f32[5,128,128]{2,1,0:T(8,128)S(1)} %get-tuple-element.6.field_ref, f32[128,128]{1,0:T(8,128)S(1)} %get-tuple-element.7.grad_ref), custom_call_target="tpu_custom_call" | custom-call | tf_op jit(solution)/shard_map/write_out/pallas_call | solution.py:316

commit v2 on v1

--- a/solution.py
+++ b/solution.py
@@ -43,7 +43,7 @@
     out_ref, grad_ref,
     adj_ref, state_ref, wake_ref, bh_ref, bl_ref, th_ref, tl_ref, ja_ref, jr_ref, js_ref, wc_ref, in_sem,
     send, recv, wsend, wrecv, wfull, back, ret, hsend, hrecv, esend, erecv, acc,
-    f_ssem, f_rsem, w_ssem, w_rsem, b_ssem, b_rsem, h_ssem, h_rsem, e_ssem, e_rsem,
+    f_ssem, f_rsem, w_ssem, w_rsem, b_ssem, b_rsem, h_ssem, h_rsem, e_ssem, e_rsem, group_sem, near_sem,
 ):
     me = lax.axis_index("mode")
     ax = lax.axis_index("ax")
@@ -54,18 +54,12 @@
     others = [lax.rem(me + i, D) for i in ORDER]
 
     barrier = pltpu.get_barrier_semaphore()
+    host = me == D - 1
     for other in others:
-        pl.semaphore_signal(barrier, inc=1, device_id={"mode": other}, device_id_type=MESH)
-
-    @pl.when(has_up)
-    def _():
-        pl.semaphore_signal(barrier, inc=1, device_id={"ax": ax + 1}, device_id_type=MESH)
-
-    @pl.when(has_down)
-    def _():
-        pl.semaphore_signal(barrier, inc=1, device_id={"ax": ax - 1}, device_id_type=MESH)
-
-    pl.semaphore_signal(barrier, inc=1, device_id={"rad": 1 - rad}, device_id_type=MESH)
+
+        @pl.when(other != D - 1)
+        def _():
+            pl.semaphore_signal(barrier, inc=1, device_id={"mode": other}, device_id_type=MESH)
 
     sources = (adj_hbm, state_hbm, wake_hbm, bh_hbm, bl_hbm, th_hbm, tl_hbm, ja_hbm, jr_hbm, js_hbm, wc_hbm)
     targets = (adj_ref, state_ref, wake_ref, bh_ref, bl_ref, th_ref, tl_ref, ja_ref, jr_ref, js_ref, wc_ref)
@@ -108,7 +102,19 @@
                 m = low_half[:q]
                 wsend[2 * x] = jnp.where(m, w[:q], w_swap[q:])
                 wsend[2 * x + 1] = jnp.where(m, w_swap[:q], w[q:])
-            pl.semaphore_wait(barrier, D + has_up.astype(jnp.int32) + has_down.astype(jnp.int32))
+
+            @pl.when(jnp.logical_not(host))
+            def _():
+                pl.semaphore_wait(barrier, D - 1)
+
+            @pl.when(me == D - 2)
+            def _():
+                pl.semaphore_signal(group_sem, inc=1, device_id={"mode": me + 1}, device_id_type=MESH)
+
+            @pl.when(host)
+            def _():
+                pl.semaphore_wait(group_sem, 1)
+
         for other in others:
             go(send.at[f, other], recv.at[f, me], f_ssem.at[f], f_rsem.at[f], {"mode": other})
         if f == 0:
@@ -126,15 +132,39 @@
             edge = jnp.where(lane == s, v, edge)
     esend[...] = edge
 
-    @pl.when(has_down)
-    def _():
-        go(hsend.at[0], hrecv.at[1], h_ssem.at[0], h_rsem.at[1], {"ax": ax - 1})
-
-    @pl.when(has_up)
-    def _():
-        go(hsend.at[1], hrecv.at[0], h_ssem.at[1], h_rsem.at[0], {"ax": ax + 1})
-
-    go(esend, erecv, e_ssem, e_rsem, {"rad": 1 - rad})
+    @pl.when(host)
+    def _():
+        pl.semaphore_signal(barrier, inc=1, device_id={"rad": 1 - rad}, device_id_type=MESH)
+
+    @pl.when(jnp.logical_and(host, has_up))
+    def _():
+        pl.semaphore_signal(barrier, inc=1, device_id={"ax": ax + 1}, device_id_type=MESH)
+
+    @pl.when(jnp.logical_and(host, has_down))
+    def _():
+        pl.semaphore_signal(barrier, inc=1, device_id={"ax": ax - 1}, device_id_type=MESH)
+
+    def tell_group():
+        @pl.when(host)
+        def _():
+            pl.semaphore_wait(barrier, 1 + has_up.astype(jnp.int32) + has_down.astype(jnp.int32))
+            for other in range(D - 1):
+                pl.semaphore_signal(near_sem, inc=1, device_id={"mode": other}, device_id_type=MESH)
+
+    def send_halos():
+        @pl.when(jnp.logical_not(host))
+        def _():
+            pl.semaphore_wait(near_sem, 1)
+
+        @pl.when(has_down)
+        def _():
+            go(hsend.at[0], hrecv.at[1], h_ssem.at[0], h_rsem.at[1], {"ax": ax - 1})
+
+        @pl.when(has_up)
+        def _():
+            go(hsend.at[1], hrecv.at[0], h_ssem.at[1], h_rsem.at[0], {"ax": ax + 1})
+
+        go(esend, erecv, e_ssem, e_rsem, {"rad": 1 - rad})
 
     wrecv[me] = wsend[me]
     for f in range(F):
@@ -161,6 +191,10 @@
     total = None
     first = None
     for f in range(F):
+        if f == F - 2:
+            tell_group()
+        if f == F - 1:
+            send_halos()
         whole(recv.at[f, seven], f_rsem.at[f]).wait_recv()
         angle = product(bh_ref[...], bl_ref[...], recv[f].reshape(D * K, L))
         angle_swap = swap(angle)
@@ -302,7 +336,7 @@
             pltpu.VMEM((K, L), f32),
             pltpu.VMEM((F, X, K, L), f32),
             dma((F,)), dma((F,)), dma, dma, dma((PAIRS,)), dma((PAIRS,)),
-            dma((2,)), dma((2,)), dma, dma,
+            dma((2,)), dma((2,)), dma, dma, pltpu.SemaphoreType.REGULAR, pltpu.SemaphoreType.REGULAR,
         ],
         compiler_params=pltpu.CompilerParams(
             collective_id=0, has_side_effects=True, vmem_limit_bytes=32 * 1024 * 1024

time: 28.2 us -> 30.6 us (1.085)
  Pallas kernels: 27.4 us -> 29.8 us
    pallas_call x1, Pallas kernels: 26.7 us -> 29.1 us  [body(): pl.pallas_call(kernel, out_shape=(jax.ShapeDtypeStruct((F, K * X, L), f32...]
where the time goes in v2:
time: 30.6 us; the launch traced here: 30.5 us
  Pallas kernels  29.8 us (97%)
  between operations  0.64 us (2%)
    pallas_call x1, Pallas kernels, body(): pl.pallas_call(kernel, out_shape=(jax.ShapeDtypeStruct((F, K * X, L), f32...  29.1 us
    pallas_call x1, Pallas kernels, body(): pl.pallas_call(write_out, out_shape=(jax.ShapeDtypeStruct((F, K * X, L),...  0.76 us

profile of v2, /device:TPU:40, one launch (start us, length us, event | category | flops | bytes accessed | tf_op | source)
XLA Modules:
  0.0 30.5 jit_solution(15731565475505213173)
XLA Ops:
  0.6 29.1 %section_adjoint.1 = (f32[5,128,128]{2,1,0:T(8,128)S(1)}, f32[128,128]{1,0:T(8,128)S(1)}) custom-call(f32[5,128,128]{2,1,0:T(8,128)} %bitcast.5, f32[5,128,128]{2,1,0:T(8,128)} %bitcast.6, f32[128,128]{1,0:T(8,128)} %bitcast.7, bf16[256,256]{1,0:T(8,128)(2,1)} %constant.8.clone.bh_hbm, bf16[256,256]{1,0:T(8,128)(2,1)} %constant.9.clone.bl_hbm, ...), custom_call_target="tpu_custom_call" | custom-call | tf_op jit(solution)/shard_map/section_adjoint/pallas_call | solution.py:311
  29.7 0.8 %write_out.1 = (f32[5,128,128]{2,1,0:T(8,128)}, f32[128,128]{1,0:T(8,128)}) custom-call(f32[5,128,128]{2,1,0:T(8,128)S(1)} %get-tuple-element.6.field_ref, f32[128,128]{1,0:T(8,128)S(1)} %get-tuple-element.7.grad_ref), custom_call_target="tpu_custom_call" | custom-call | tf_op jit(solution)/shard_map/write_out/pallas_call | solution.py:350

commit v3 on v1

--- a/solution.py
+++ b/solution.py
@@ -44,6 +44,7 @@
     adj_ref, state_ref, wake_ref, bh_ref, bl_ref, th_ref, tl_ref, ja_ref, jr_ref, js_ref, wc_ref, in_sem,
     send, recv, wsend, wrecv, wfull, back, ret, hsend, hrecv, esend, erecv, acc,
     f_ssem, f_rsem, w_ssem, w_rsem, b_ssem, b_rsem, h_ssem, h_rsem, e_ssem, e_rsem,
+    relay, brelay, r_rsem, br_rsem, fw_ssem, fb_ssem,
 ):
     me = lax.axis_index("mode")
     ax = lax.axis_index("ax")
@@ -52,6 +53,11 @@
     has_up = ax < ax_count - 1
     has_down = ax > 0
     others = [lax.rem(me + i, D) for i in ORDER]
+    core = lax.rem(me, 2)
+    ahead = lax.rem(me - core + 2, D)
+    behind = lax.rem(me - core + D - 2, D)
+    away = lax.rem(me - core + 4, D)
+    direct = [ahead + core, behind + core, ahead + 1 - core, behind + 1 - core, me + 1 - 2 * core]
 
     barrier = pltpu.get_barrier_semaphore()
     for other in others:
@@ -88,6 +94,24 @@
         )
         copy.start()
         return copy
+
+    def whole(ref, sem):
+        return pltpu.make_async_remote_copy(
+            src_ref=ref, dst_ref=ref, send_sem=sem, recv_sem=sem, device_id={"rad": 1 - rad}, device_id_type=MESH
+        )
+
+    def to_relay(src, dst, ssem, rsem):
+        go(src.at[away], dst.at[0], ssem, rsem, {"mode": ahead + core})
+        go(src.at[away + 1], dst.at[1], ssem, rsem, {"mode": behind + core})
+
+    def to_near(src, dst, ssem, rsem):
+        for other in direct:
+            go(src.at[other], dst.at[me], ssem, rsem, {"mode": other})
+
+    def forward(src, dst, arrival, ssem, rsem):
+        whole(src, arrival).wait_recv()
+        go(src.at[0], dst.at[behind + core], ssem, rsem, {"mode": ahead})
+        go(src.at[1], dst.at[ahead + core], ssem, rsem, {"mode": behind + 1})
 
     for i in (10, 1, 0):
         loads[i].wait()
@@ -109,9 +133,9 @@
                 wsend[2 * x] = jnp.where(m, w[:q], w_swap[q:])
                 wsend[2 * x + 1] = jnp.where(m, w_swap[:q], w[q:])
             pl.semaphore_wait(barrier, D + has_up.astype(jnp.int32) + has_down.astype(jnp.int32))
-        for other in others:
-            go(send.at[f, other], recv.at[f, me], f_ssem.at[f], f_rsem.at[f], {"mode": other})
+        to_relay(send.at[f], relay.at[f], f_ssem.at[f], r_rsem.at[f])
         if f == 0:
+            to_near(send.at[f], recv.at[f], f_ssem.at[f], f_rsem.at[f])
             for other in others:
                 go(wsend.at[other], wrecv.at[me], w_ssem, w_rsem, {"mode": other})
 
@@ -136,14 +160,14 @@
 
     go(esend, erecv, e_ssem, e_rsem, {"rad": 1 - rad})
 
+    for f in range(F):
+        forward(relay.at[f], recv.at[f], r_rsem.at[f], fw_ssem, f_rsem.at[f])
+        if f < F - 1:
+            to_near(send.at[f + 1], recv.at[f + 1], f_ssem.at[f + 1], f_rsem.at[f + 1])
+
     wrecv[me] = wsend[me]
     for f in range(F):
         recv[f, me] = send[f, me]
-
-    def whole(ref, sem):
-        return pltpu.make_async_remote_copy(
-            src_ref=ref, dst_ref=ref, send_sem=sem, recv_sem=sem, device_id={"rad": 1 - rad}, device_id_type=MESH
-        )
 
     seven = pl.ds(0, D - 1)
 
@@ -157,6 +181,9 @@
 
     for i in (3, 4, 5, 6, 7, 8, 9):
         loads[i].wait()
+    def forward_back(p):
+        forward(brelay.at[p], ret.at[p], br_rsem.at[p], fb_ssem, b_rsem.at[p])
+
     low_all = lax.broadcasted_iota(jnp.int32, (D * K, L), 1) < HALF
     total = None
     first = None
@@ -179,8 +206,10 @@
         if f == F - 1:
             result = jnp.where(low_all, result, -total)
         back[p] = result.reshape(D, K, L)
-        for other in others:
-            go(back.at[p, other], ret.at[p, me], b_ssem.at[p], b_rsem.at[p], {"mode": other})
+        to_relay(back.at[p], brelay.at[p], b_ssem.at[p], br_rsem.at[p])
+        to_near(back.at[p], ret.at[p], b_ssem.at[p], b_rsem.at[p])
+        if p:
+            forward_back(p - 1)
         ret[p, me] = back[p, me]
 
     @pl.when(has_down)
@@ -233,6 +262,9 @@
                 v = v + ja_ref[e, f] * axial[e] + jr_ref[e, f] * radial[e] + js_ref[e, f] * turned[e]
             acc[f, x] = v
 
+    forward_back(PAIRS - 1)
+    whole(relay, fw_ssem).wait_send()
+
     def pair(p, x):
         one, two = ret[p, 2 * x], ret[p, 2 * x + 1]
         return jnp.where(low_half, one, swap(two)), jnp.where(low_half, swap(one), two)
@@ -248,6 +280,7 @@
                 v = v - wc_ref[e, f] * returned[e]
             acc[f, x] = v
     p = PAIRS - 1
+    whole(brelay, fb_ssem).wait_send()
     whole(back.at[p, seven], b_ssem.at[p]).wait_send()
     whole(ret.at[p, seven], b_rsem.at[p]).wait_recv()
     for x in range(X):
@@ -303,6 +336,9 @@
             pltpu.VMEM((F, X, K, L), f32),
             dma((F,)), dma((F,)), dma, dma, dma((PAIRS,)), dma((PAIRS,)),
             dma((2,)), dma((2,)), dma, dma,
+            pltpu.VMEM((F, 2, K, L), f32),
+            pltpu.VMEM((PAIRS, 2, K, L), f32),
+            dma((F,)), dma((PAIRS,)), dma, dma,
         ],
         compiler_params=pltpu.CompilerParams(
             collective_id=0, has_side_effects=True, vmem_limit_bytes=32 * 1024 * 1024

time: 28.2 us -> 32.6 us (1.16)
  Pallas kernels: 27.4 us -> 31.8 us
    pallas_call x1, Pallas kernels: 26.7 us -> 31 us  [body(): pl.pallas_call(kernel, out_shape=(jax.ShapeDtypeStruct((F, K * X, L), f32...]
where the time goes in v3:
time: 32.6 us; the launch traced here: 32.4 us
  Pallas kernels  31.8 us (98%)
  between operations  0.64 us (2%)
    pallas_call x1, Pallas kernels, body(): pl.pallas_call(kernel, out_shape=(jax.ShapeDtypeStruct((F, K * X, L), f32...  31 us
    pallas_call x1, Pallas kernels, body(): pl.pallas_call(write_out, out_shape=(jax.ShapeDtypeStruct((F, K * X, L),...  0.76 us

profile of v3, /device:TPU:40, one launch (start us, length us, event | category | flops | bytes accessed | tf_op | source)
XLA Modules:
  0.0 32.4 jit_solution(5104760131868018049)
XLA Ops:
  0.6 31.0 %section_adjoint.1 = (f32[5,128,128]{2,1,0:T(8,128)S(1)}, f32[128,128]{1,0:T(8,128)S(1)}) custom-call(f32[5,128,128]{2,1,0:T(8,128)} %bitcast.5, f32[5,128,128]{2,1,0:T(8,128)} %bitcast.6, f32[128,128]{1,0:T(8,128)} %bitcast.7, bf16[256,256]{1,0:T(8,128)(2,1)} %constant.8.clone.bh_hbm, bf16[256,256]{1,0:T(8,128)(2,1)} %constant.9.clone.bl_hbm, ...), custom_call_target="tpu_custom_call" | custom-call | tf_op jit(solution)/shard_map/section_adjoint/pallas_call | solution.py:310
  31.7 0.8 %write_out.1 = (f32[5,128,128]{2,1,0:T(8,128)}, f32[128,128]{1,0:T(8,128)}) custom-call(f32[5,128,128]{2,1,0:T(8,128)S(1)} %get-tuple-element.6.field_ref, f32[128,128]{1,0:T(8,128)S(1)} %get-tuple-element.7.grad_ref), custom_call_target="tpu_custom_call" | custom-call | tf_op jit(solution)/shard_map/write_out/pallas_call | solution.py:352

commit v4 on v1

--- a/solution.py
+++ b/solution.py
@@ -175,9 +175,22 @@
             both = jnp.where(low_all, first, wake_all * angle_swap)
         else:
             both = wake_all * angle
+        if f == F - 1:
+            n = D * K // 2
+            for part in range(2):
+                rows = pl.ds(part * n, n)
+                result = product(th_ref[rows, :], tl_ref[rows, :], both)
+                result = jnp.where(low_all[:n], result, -total[part * n : (part + 1) * n])
+                back[p, pl.ds(part * D // 2, D // 2)] = result.reshape(D // 2, K, L)
+                for d in range(part * D // 2, (part + 1) * D // 2):
+
+                    @pl.when(me != d)
+                    def _():
+                        go(back.at[p, d], ret.at[p, me], b_ssem.at[p], b_rsem.at[p], {"mode": d})
+
+            ret[p, me] = back[p, me]
+            break
         result = product(th_ref[...], tl_ref[...], both)
-        if f == F - 1:
-            result = jnp.where(low_all, result, -total)
         back[p] = result.reshape(D, K, L)
         for other in others:
             go(back.at[p, other], ret.at[p, me], b_ssem.at[p], b_rsem.at[p], {"mode": other})

time: 28.2 us -> 28.2 us (level); the launches traced: 28.1 us -> 27.7 us
  Pallas kernels: 27.4 us -> 27.1 us
    pallas_call x1, Pallas kernels: 26.7 us -> 26.3 us  [body(): pl.pallas_call(kernel, out_shape=(jax.ShapeDtypeStruct((F, K * X, L), f32...]
where the time goes in v4:
time: 28.2 us; the launch traced here: 27.7 us
  Pallas kernels  27.1 us (96%)
  between operations  0.64 us (2%)
    pallas_call x1, Pallas kernels, body(): pl.pallas_call(kernel, out_shape=(jax.ShapeDtypeStruct((F, K * X, L), f32...  26.3 us
    pallas_call x1, Pallas kernels, body(): pl.pallas_call(write_out, out_shape=(jax.ShapeDtypeStruct((F, K * X, L),...  0.76 us

profile of v4, /device:TPU:40, one launch (start us, length us, event | category | flops | bytes accessed | tf_op | source)
XLA Modules:
  0.0 27.7 jit_solution(17310652292805954178)
XLA Ops:
  0.6 26.3 %section_adjoint.1 = (f32[5,128,128]{2,1,0:T(8,128)S(1)}, f32[128,128]{1,0:T(8,128)S(1)}) custom-call(f32[5,128,128]{2,1,0:T(8,128)} %bitcast.5, f32[5,128,128]{2,1,0:T(8,128)} %bitcast.6, f32[128,128]{1,0:T(8,128)} %bitcast.7, bf16[256,256]{1,0:T(8,128)(2,1)} %constant.8.clone.bh_hbm, bf16[256,256]{1,0:T(8,128)(2,1)} %constant.9.clone.bl_hbm, ...), custom_call_target="tpu_custom_call" | custom-call | tf_op jit(solution)/shard_map/section_adjoint/pallas_call | solution.py:290
  27.0 0.8 %write_out.1 = (f32[5,128,128]{2,1,0:T(8,128)}, f32[128,128]{1,0:T(8,128)}) custom-call(f32[5,128,128]{2,1,0:T(8,128)S(1)} %get-tuple-element.6.field_ref, f32[128,128]{1,0:T(8,128)S(1)} %get-tuple-element.7.grad_ref), custom_call_target="tpu_custom_call" | custom-call | tf_op jit(solution)/shard_map/write_out/pallas_call | solution.py:329
